TPU v7x, 256 devices: a whole 4x4x8 slice. The times are simulated.
256 devices in a mesh: row: 8 (over x_hi, y), col: 16 (over x_lo, z), depth: 2 (over core).
Axes of the slice: x: 4 (x_hi: 2, x_lo: 2; x = x_hi * 2 + x_lo), y: 4, z: 8, core: 2. Of those that a mesh axis runs over, the one named last changes fastest.
Arguments:
- snapshots: bfloat16 [8192, 6144], P('col', ('row', 'depth')), may hold values from -6 to 6
- cell_weight: float32 [6144], P(('row', 'depth')), may hold values from 0.25 to 4
Outputs:
- gram: float32 [8192, 8192], P('row', ('col', 'depth'))
All inputs are finite; a program needn't handle non-finite values.
Results may differ from a plain program's by a relative error of at most 0.0034.
Values may be sent and summed in bfloat16 or wider, within the bound.
A program may use at most 64 MiB of HBM per device.

v0:
```python
import jax
import jax.numpy as jnp
from jax import lax
from jax.sharding import PartitionSpec as P

CELLS = 6144


def spread(value, axis, root):
    mine = lax.axis_index(axis) == root
    return lax.psum(jnp.where(mine, value, jnp.zeros_like(value)), axis)


def block_product(left_rows, right_rows):
    return lax.dot_general(
        left_rows, right_rows, (((1,), (1,)), ((), ())), preferred_element_type=jnp.float32
    )


def on_device(snapshots, cell_weight):
    root_weight = jnp.sqrt(cell_weight)
    scaled = (snapshots.astype(jnp.float32) * root_weight[None, :]).astype(jnp.bfloat16)
    ratio = lax.axis_size("col") // lax.axis_size("row")
    row_index = lax.axis_index("row")
    own_half = lax.all_to_all(scaled, "depth", split_axis=0, concat_axis=1, tiled=True)
    column_rows = lax.all_gather(own_half, "row", axis=1, tiled=True)
    blocks = []
    for offset in range(ratio):
        received = spread(column_rows, "col", row_index * ratio + offset)
        panel = lax.all_gather(received, "depth", axis=0, tiled=True)
        blocks.append(block_product(panel, column_rows))
    summed = jnp.concatenate(blocks, axis=0)
    return summed / jnp.float32(CELLS)


def solution(mesh):
    return jax.shard_map(
        on_device,
        mesh=mesh,
        in_specs=(P("col", ("row", "depth")), P(("row", "depth"))),
        out_specs=P("row", ("col", "depth")),
        check_vma=False,
    )
```

profile of v0, /device:TPU:1, one launch (start us, length us, event | category | flops | bytes accessed | tf_op | source)
XLA Modules:
  0.0 312.5 jit_solution(17423698580459638901)
XLA Ops:
  6.5 0.0 all-gather.4.cloned.1.call-start
  6.5 0.7 sqrt.3
  7.2 1.1 multiply_convert_fusion
  8.3 6.9 %all_to_all.19 = bf16[2,256,384]{2,1,0:T(8,128)(2,1)S(1)} all-to-all(bf16[2,256,384]{2,1,0:T(8,128)(2,1)S(1)} %bitcast.8), channel_id=1, replica_groups=mesh['row'=8,'col'=16,'depth'=2] {'depth'}, dimensions={0} | all-to-all | bytes 786432 | tf_op jit(solution)/shard_map/all_to_all | solution.py:25
  15.2 0.9 copy.3
  16.1 0.0 all-gather.4.cloned.1.call-update
  16.2 0.0 all-reduce.3.cloned.1.call-start
  16.2 68.3 %all-gather.4.cloned.1.call-done = bf16[256,6144]{0,1:T(8,128)(2,1)} async-done(((bf16[256,768]{0,1:T(8,128)(2,1)}), bf16[256,6144]{0,1:T(8,128)(2,1)}) %all-gather.4.cloned.1.call-update) | async-done | bytes 3145744 | tf_op jit(solution)/shard_map/all_gather | solution.py:26
  84.6 4.9 %broadcast_select_fusion.1 = (bf16[256,6144]{0,1:T(8,128)(2,1)}, bf16[256,6144]{0,1:T(8,128)(2,1)}) fusion(bf16[256,6144]{0,1:T(8,128)(2,1)} %all-gather.4.cloned.1.call-done, pred[]{:T(512)S(6)} %eq.6, pred[]{:T(512)S(6)} %eq.7), kind=kLoop, calls=%fused_computation.1 | loop fusion | flops 3145728 | bytes 9437186 | tf_op jit(solution)/shard_map/jit(_where)/select_n | solution.py:11
  89.5 0.0 all-reduce.3.cloned.1.call-update
  89.5 0.0 all-gather.8.cloned.1.call-start
  89.6 162.2 %all-reduce.3.cloned.1.call-done = (bf16[256,6144]{0,1:T(8,128)(2,1)}, bf16[256,6144]{0,1:T(8,128)(2,1)}) async-done(((bf16[256,6144]{0,1:T(8,128)(2,1)}, bf16[256,6144]{0,1:T(8,128)(2,1)}), (bf16[256,6144]{0,1:T(8,128)(2,1)}, bf16[256,6144]{0,1:T(8,128)(2,1)})) %all-reduce.3.cloned.1.call-update) | async-done | bytes 6291472 | tf_op jit(solution)/shard_map/psum | solution.py:11
  251.7 0.0 copy-start
  251.7 0.0 all-gather.8.cloned.1.call-update
  251.8 0.0 all-gather.6.cloned.1.call-start
  251.8 0.5 all-gather.6.cloned.1.call-update
  252.3 23.9 %all-gather.8.cloned.1.call-done = bf16[512,6144]{0,1:T(8,128)(2,1)} async-done(((bf16[256,6144]{0,1:T(8,128)(2,1)}), bf16[512,6144]{0,1:T(8,128)(2,1)}) %all-gather.8.cloned.1.call-update) | async-done | bytes 6291472 | tf_op jit(solution)/shard_map/all_gather | solution.py:30
  276.3 0.0 copy-done
  276.3 5.4 %fusion.1 = f32[512,256]{1,0:T(8,128)} fusion(bf16[512,6144]{0,1:T(8,128)(2,1)} %all-gather.8.cloned.1.call-done, bf16[256,6144]{0,1:T(8,128)(2,1)S(1)} %copy-done), kind=kOutput, calls=%fused_computation.5 | convolution fusion | flops 1610612736 | bytes 9961472 | tf_op jit(solution)/shard_map/dot_general | solution.py:15
  281.7 18.6 %all-gather.6.cloned.1.call-done = bf16[512,6144]{0,1:T(8,128)(2,1)} async-done(((bf16[256,6144]{0,1:T(8,128)(2,1)}), bf16[512,6144]{0,1:T(8,128)(2,1)}) %all-gather.6.cloned.1.call-update) | async-done | bytes 6291472 | tf_op jit(solution)/shard_map/all_gather | solution.py:30
  300.2 0.0 copy-start.1
  300.2 4.7 %fusion = f32[512,256]{1,0:T(8,128)S(1)} fusion(bf16[512,6144]{0,1:T(8,128)(2,1)} %all-gather.6.cloned.1.call-done, bf16[256,6144]{0,1:T(8,128)(2,1)S(1)} %copy-done), kind=kOutput, calls=%fused_computation.4 | convolution fusion | flops 1610612736 | bytes 9961472 | tf_op jit(solution)/shard_map/dot_general | solution.py:15
  304.9 0.0 copy-done.1
  304.9 1.1 maximum_multiply_fusion
Async XLA Ops:
  6.5 78.0 %all-gather.4.cloned.1.call-start = ((), (), s32[]{:S(2)}) async-start(), calls=%async_computation.1 | async-start | bytes 3538944 | tf_op jit(solution)/shard_map/all_gather | solution.py:26
  16.2 235.6 %all-reduce.3.cloned.1.call-start = ((), (), s32[]{:S(2)}) async-start(), calls=%async_computation.4 | async-start | bytes 12582912 | tf_op jit(solution)/shard_map/psum | solution.py:11
  89.5 186.7 %all-gather.8.cloned.1.call-start = ((), (), s32[]{:S(2)}) async-start(), calls=%async_computation.3 | async-start | bytes 9437184 | tf_op jit(solution)/shard_map/all_gather | solution.py:30
  251.7 24.5 %copy-start = (bf16[256,6144]{0,1:T(8,128)(2,1)S(1)}, bf16[256,6144]{0,1:T(8,128)(2,1)}, u32[]{:S(2)}) copy-start(bf16[256,6144]{0,1:T(8,128)(2,1)} %all-gather.4.cloned.1.call-done) | copy-start | bytes 9437188
  251.8 48.5 %all-gather.6.cloned.1.call-start = ((), (), s32[]{:S(2)}) async-start(), calls=%async_computation.2 | async-start | bytes 9437184 | tf_op jit(solution)/shard_map/all_gather | solution.py:30
  300.2 4.7 %copy-start.1 = (f32[512,256]{1,0:T(8,128)S(1)}, f32[512,256]{1,0:T(8,128)}, u32[]{:S(2)}) copy-start(f32[512,256]{1,0:T(8,128)} %fusion.1) | copy-start | bytes 1572868
Sparse Core Ops, SparseCore 0:
  16.3 68.2 all-gather.3
  89.6 162.0 all-reduce.2
  253.5 22.6 all-gather.7
  277.9 22.2 all-gather.5
where the time goes:
time: 313 us
  waiting for transfers between devices  274 us (88%)
  between operations  13.2 us (4%)
  matrix products  10.1 us (3%)
  other arithmetic  7.09 us (2%)
  blocking collectives  6.92 us (2%)
    psum x1, waiting for transfers between devices, spread(): return lax.psum(jnp.where(mine, value, jnp.zeros_like(value)), axis)  162 us
    all_gather x1, waiting for transfers between devices, on_device(): column_rows = lax.all_gather(own_half, 'row', axis=1, tiled=True)  68.3 us
    all_gather x2, waiting for transfers between devices, on_device(): panel = lax.all_gather(received, 'depth', axis=0, tiled=True)  42.5 us
    dot_general x2, matrix products, block_product(): lax.dot_general(left_rows, right_rows, (((1,), (1,)), ((), ())), preferre...  10.1 us
    all_to_all x1, blocking collectives, on_device(): lax.all_to_all(scaled, 'depth', split_axis=0, concat_axis=1, tiled=True)  6.92 us
  transfers between devices with their start and end apart: 4, of which 4 were waited for; matrix products, arithmetic and copies ran while one was open for 2% of the time, Pallas kernels for 0%

commit v1 on v0

v1 whole, which is shorter than its diff:
```python
import functools

import jax
import jax.numpy as jnp
from jax import lax
from jax.experimental import pallas as pl
from jax.experimental.pallas import tpu as pltpu
from jax.sharding import PartitionSpec as P

MESH = pl.DeviceIdType.MESH
CELLS = 6144
SNAP = 512
CELL = 384
PART = 64
COLS = 256


def kernel(
    snap_ref, weight_ref, out_ref, own, cols, rows, partial, peer, half_out, half_in,
    a_send, a_recv, x_send, x_recv, y_send, y_recv, f_send, f_recv,
    z_send, z_recv, p_send, p_recv, q_send, q_recv,
):
    row, col, d = lax.axis_index("row"), lax.axis_index("col"), lax.axis_index("depth")
    h, y, l, z = row // 4, lax.rem(row, 4), col // 8, lax.rem(col, 8)

    def device(h, l, y, z, d):
        return (h * 4 + y, l * 8 + z, d)

    def turn(value, by, size):
        return lax.rem(value + by + size, size)

    up_y, down_y = device(h, l, turn(y, 1, 4), z, d), device(h, l, turn(y, -1, 4), z, d)
    up_z, down_z = device(h, l, y, turn(z, 1, 8), d), device(h, l, y, turn(z, -1, 8), d)
    sibling = device(h, l, y, z, 1 - d)
    partner = device(h, 1 - l, y, z, d)

    barrier = pltpu.get_barrier_semaphore()

    def greet(target):
        pl.semaphore_signal(barrier, inc=1, device_id=target, device_id_type=MESH)

    for target in (up_y, down_y, up_z, down_z, sibling, partner):
        greet(target)
    for block in range(2):
        greet(device(l, block, y, z, d))
        for part_y in range(4):
            greet(device(l, h, part_y, 2 * y + block, d))

    root = jnp.sqrt(weight_ref[...])
    own[...] = (snap_ref[...].astype(jnp.float32) * root[None, :]).astype(jnp.bfloat16)
    pl.semaphore_wait(barrier, 16)

    def remote(src, dst, send, recv, target):
        return pltpu.make_async_remote_copy(
            src_ref=src, dst_ref=dst, send_sem=send, recv_sem=recv, device_id=target, device_id_type=MESH
        )

    def sub_at(piece, sub):
        return rows.at[piece, pl.ds((sub // 4) * PART, PART), pl.ds((sub % 4) * CELL, CELL)]

    def block_at(which, cell_y):
        return cols.at[pl.ds(which * SNAP, SNAP), pl.ds(pl.multiple_of(cell_y * CELL, CELL), CELL)]

    half = lax.rem(z, 2)
    ring_y = z // 2
    a_index = half * 4 + y
    same_ring = (h == l) & (y == ring_y)

    def a_parts(p):
        src = own.at[pl.ds(p * PART, PART), :]
        dst = rows.at[
            p, pl.ds(pl.multiple_of(half * PART, PART), PART), pl.ds(pl.multiple_of(y * CELL, CELL), CELL)
        ]
        return src, dst

    def a_copy(p):
        src, dst = a_parts(p)
        return remote(src, dst, a_send.at[p], a_recv.at[a_index], device(l, h, ring_y, p, d))

    for p in range(8):
        to_self = same_ring & (z == p)

        @pl.when(to_self)
        def _():
            src, dst = a_parts(p)
            pltpu.make_async_copy(src, dst, a_recv.at[a_index]).start()

        @pl.when(jnp.logical_not(to_self))
        def _():
            a_copy(p).start()

    def x_copy(to):
        return remote(own, block_at(l, y), x_send.at[to], x_recv.at[l], device(to, h, y, z, d))

    for to in range(2):
        to_self = (h == to) & (l == h)

        @pl.when(to_self)
        def _():
            pltpu.make_async_copy(own, block_at(l, y), x_recv.at[l]).start()

        @pl.when(jnp.logical_not(to_self))
        def _():
            x_copy(to).start()

    def y_copy(way, which):
        return remote(
            block_at(which, y), block_at(which, y), y_send.at[way, which], y_recv.at[way, which],
            (up_y, down_y)[way],
        )

    def y_arrival(way, which):
        at = block_at(which, turn(y, (-1, 1)[way], 4))
        return remote(at, at, y_send.at[way, which], y_recv.at[way, which], (up_y, down_y)[way])

    def forward_copy(way):
        at = block_at(way, turn(y, (-1, 1)[way], 4))
        return remote(at, at, f_send.at[way], f_recv.at[way], (up_y, down_y)[way])

    def forward_arrival(way):
        at = block_at(way, turn(y, 2, 4))
        return remote(at, at, f_send.at[way], f_recv.at[way], (up_y, down_y)[way])

    def z_copy(way, hop, sub):
        at = sub_at(turn(z, (-hop, hop)[way], 8), sub)
        return remote(at, at, z_send.at[way, hop, sub], z_recv.at[way, hop, sub], (up_z, down_z)[way])

    def z_arrival(way, hop, sub):
        at = sub_at(turn(z, (-hop, hop)[way], 8), sub)
        return remote(at, at, z_send.at[way, hop - 1, sub], z_recv.at[way, hop - 1, sub], (up_z, down_z)[way])

    def x_wait(which):
        at = block_at(which, y)
        remote(at, at, x_send.at[0], x_recv.at[which], partner).wait_recv()
        for way in range(2):
            y_copy(way, which).start()

    for sub in range(8):
        at = sub_at(z, sub)
        remote(at, at, a_send.at[0], a_recv.at[sub], partner).wait_recv()
        for way in range(2):
            z_copy(way, 0, sub).start()
        if sub == 3:
            x_wait(0)
    x_wait(1)

    for hop in range(1, 4):
        for sub in range(8):
            for way in range(2):
                z_arrival(way, hop, sub).wait_recv()
                if hop < 3 or sub // 4 == way:
                    z_copy(way, hop, sub).start()
        if hop == 1:
            for way in range(2):
                y_arrival(way, way).wait_recv()
                forward_copy(way).start()
    for way in range(2):
        y_arrival(way, 1 - way).wait_recv()
        forward_arrival(way).wait_recv()

    def piece_of(step):
        behind = lax.rem(step, 2)
        off = (step + 1) // 2
        return lax.rem(z + 8 + jnp.where(behind == 1, -off, off), 8)

    def peer_copy(step):
        return remote(partial.at[step, 1 - d], peer.at[step], p_send.at[step], p_recv.at[step], sibling)

    def half_copy(step):
        return remote(half_out.at[step], half_in.at[step], q_send.at[step], q_recv.at[step], partner)

    def multiply(step):
        left = rows[piece_of(step)]
        for which in range(2):
            for side in range(2):
                right = cols[pl.ds(which * SNAP + side * COLS, COLS), :]
                partial[step, side, which] = lax.dot_general(
                    left, right, (((1,), (1,)), ((), ())), preferred_element_type=jnp.float32
                )
        peer_copy(step).start()

    def sum_cores(step):
        peer_copy(step).wait_recv()
        half_out[step] = (partial[step, d, 1 - l] + peer[step, 1 - l]).astype(jnp.bfloat16)
        half_copy(step).start()

    def sum_chips(step):
        half_copy(step).wait_recv()
        total = partial[step, d, l] + peer[step, l] + half_in[step].astype(jnp.float32)
        total = total * jnp.float32(1.0 / CELLS)
        at = pl.multiple_of(piece_of(step) * PART, PART)
        out_ref[pl.ds(at, PART), :] = total[:PART]
        out_ref[pl.ds(SNAP + at, PART), :] = total[PART:]

    @pl.loop(0, 10)
    def _(step):
        @pl.when(step == 7)
        def _():
            for sub in range(8):
                z_arrival(sub // 4, 4, sub).wait_recv()

        @pl.when(step < 8)
        def _():
            multiply(step)

        @pl.when((step >= 1) & (step < 9))
        def _():
            sum_cores(step - 1)

        @pl.when(step >= 2)
        def _():
            sum_chips(step - 2)

    for p in range(8):

        @pl.when(jnp.logical_not(same_ring & (z == p)))
        def _():
            a_copy(p).wait_send()

    for to in range(2):

        @pl.when(jnp.logical_not((h == to) & (l == h)))
        def _():
            x_copy(to).wait_send()

    for way in range(2):
        for which in range(2):
            y_copy(way, which).wait_send()
        forward_copy(way).wait_send()
        for hop in range(4):
            for sub in range(8):
                if hop < 3 or sub // 4 == way:
                    z_copy(way, hop, sub).wait_send()
    for step in range(8):
        peer_copy(step).wait_send()
        half_copy(step).wait_send()


def on_device(snapshots, cell_weight):
    vmem = pl.BlockSpec(memory_space=pltpu.VMEM)
    dma = pltpu.SemaphoreType.DMA
    return pl.pallas_call(
        kernel,
        out_shape=jax.ShapeDtypeStruct((2 * SNAP, COLS), jnp.float32),
        in_specs=[vmem, vmem],
        out_specs=vmem,
        scratch_shapes=[
            pltpu.VMEM((SNAP, CELL), jnp.bfloat16),
            pltpu.VMEM((2 * SNAP, 4 * CELL), jnp.bfloat16),
            pltpu.VMEM((8, 2 * PART, 4 * CELL), jnp.bfloat16),
            pltpu.VMEM((8, 2, 2, 2 * PART, COLS), jnp.float32),
            pltpu.VMEM((8, 2, 2 * PART, COLS), jnp.float32),
            pltpu.VMEM((8, 2 * PART, COLS), jnp.bfloat16),
            pltpu.VMEM((8, 2 * PART, COLS), jnp.bfloat16),
            dma((8,)), dma((8,)), dma((2,)), dma((2,)), dma((2, 2)), dma((2, 2)), dma((2,)), dma((2,)),
            dma((2, 4, 8)), dma((2, 4, 8)), dma((8,)), dma((8,)), dma((8,)), dma((8,)),
        ],
        compiler_params=pltpu.CompilerParams(
            collective_id=0, has_side_effects=True, vmem_limit_bytes=48 << 20
        ),
        name="gram",
    )(snapshots, cell_weight)


def solution(mesh):
    return jax.shard_map(
        on_device,
        mesh=mesh,
        in_specs=(P("col", ("row", "depth")), P(("row", "depth"))),
        out_specs=P("row", ("col", "depth")),
        check_vma=False,
    )
```

time: 313 us -> 91.1 us (0.29)
  waiting for transfers between devices: 274 us -> 0 us
  Pallas kernels: 0 us -> 88.3 us
  between operations: 13.2 us -> 0.01 us
  matrix products: 10.1 us -> 0 us
  other arithmetic: 7.09 us -> 0 us
  blocking collectives: 6.92 us -> 0 us
    psum x1 -> x0, waiting for transfers between devices: 162 us -> none  [spread(): return lax.psum(jnp.where(mine, value, jnp.zeros_like(value)), axis)]
    all_gather x3 -> x0, waiting for transfers between devices: 111 us -> none  [the longest x1 68.3 us: on_device(): column_rows = lax.all_gather(own_half, 'row', axis=1, tiled=True)]
    pallas_call x0 -> x1, Pallas kernels: none -> 88.3 us  [on_device(): pl.pallas_call(kernel, out_shape=jax.ShapeDtypeStruct((2 * SNAP, COLS), j...]
    dot_general x2 -> x0, matrix products: 10.1 us -> none  [block_product(): lax.dot_general(left_rows, right_rows, (((1,), (1,)), ((), ())), preferre...]
    all_to_all x1 -> x0, blocking collectives: 6.92 us -> none  [on_device(): lax.all_to_all(scaled, 'depth', split_axis=0, concat_axis=1, tiled=True)]
    select_n x1 -> x0, other arithmetic: 4.94 us -> none  [spread(): return lax.psum(jnp.where(mine, value, jnp.zeros_like(value)), axis)]
  transfers between devices with their start and end apart: 4 -> 0, of which waited for: 4 -> 0; matrix products, arithmetic and copies ran while one was open for 2% -> 0% of each run, Pallas kernels for 0% -> 0%
where the time goes in v1:
time: 91.1 us; the launch traced here: 91 us
  Pallas kernels  88.3 us (97%)
  local copies, waits for them, and re-layouts  2.65 us (3%)
    pallas_call x1, Pallas kernels, on_device(): pl.pallas_call(kernel, out_shape=jax.ShapeDtypeStruct((2 * SNAP, COLS), j...  88.3 us
    unnamed x5, local copies, waits for them, and re-layouts  2.65 us

profile of v1, /device:TPU:1, one launch (start us, length us, event | category | flops | bytes accessed | tf_op | source)
XLA Modules:
  0.0 91.0 jit_solution(13509127454252910998)
XLA Ops:
  0.0 0.0 copy-start
  0.0 1.0 %copy-done = bf16[512,384]{1,0:T(8,128)(2,1)S(1)} copy-done((bf16[512,384]{1,0:T(8,128)(2,1)S(1)}, bf16[512,384]{1,0:T(8,128)(2,1)}, u32[]{:S(2)}) %copy-start) | copy-done | bytes 393240
  1.0 0.0 copy-start.1
  1.0 0.7 copy-done.1
  1.7 88.3 %gram.1 = f32[1024,256]{1,0:T(8,128)S(1)} custom-call(bf16[512,384]{1,0:T(8,128)(2,1)S(1)} %copy-done, f32[384]{0:T(512)S(1)} %copy-done.1), custom_call_target="tpu_custom_call" | custom-call | tf_op jit(solution)/shard_map/gram/pallas_call | solution.py:242
  90.0 1.0 %copy.4 = f32[1024,256]{1,0:T(8,128)} copy(f32[1024,256]{1,0:T(8,128)S(1)} %gram.1) | data formatting | bytes 2097152
Async XLA Ops:
  0.0 1.0 %copy-start = (bf16[512,384]{1,0:T(8,128)(2,1)S(1)}, bf16[512,384]{1,0:T(8,128)(2,1)}, u32[]{:S(2)}) copy-start(bf16[512,384]{1,0:T(8,128)(2,1)} %snap_ref.1) | copy-start | bytes 1179652
  1.0 0.7 copy-start.1

commit v2 on v0

v2 whole, which is shorter than its diff:
```python
import jax
import jax.numpy as jnp
from jax import lax
from jax.experimental import pallas as pl
from jax.experimental.pallas import tpu as pltpu
from jax.sharding import PartitionSpec as P

MESH = pl.DeviceIdType.MESH
CELLS = 6144
SNAP = 512
CELL = 384
PART = 64
PIECE = 2 * PART
COLS = 256
CHUNK = 128
CHUNKS = SNAP // CHUNK

OWN, OPPOSITE, HOP1, HOP2, HOP3 = (0, 1), (1, 1), (2, 2), (4, 2), (6, 2)
GROUPS = (OWN, HOP1, HOP2, HOP3, OPPOSITE)


def kernel(
    snap_ref, weight_ref, out_ref, raw, weight, own, relay, cols, rows, partial, peer, half_out, half_in,
    in_sem, a_send, a_recv, r_recv, x_send, x_recv, y_send, y_recv, f_send, f_recv,
    z_send, z_recv, p_send, p_recv, q_send, q_recv,
):
    row, col, d = lax.axis_index("row"), lax.axis_index("col"), lax.axis_index("depth")
    h, y, l, z = row // 4, lax.rem(row, 4), col // 8, lax.rem(col, 8)

    def device(h, l, y, z, d):
        return (h * 4 + y, l * 8 + z, d)

    def turn(value, by, size):
        return lax.rem(value + by + size, size)

    along_y = [device(h, l, turn(y, by, 4), z, d) for by in (1, -1)]
    along_z = [device(h, l, y, turn(z, by, 8), d) for by in (1, -1)]
    sibling = device(h, l, y, z, 1 - d)
    partner = device(h, 1 - l, y, z, d)
    opposite = device(1 - h, 1 - l, y, z, d)
    outer = h == l
    inner = h != l

    load = [
        pltpu.make_async_copy(snap_ref, raw, in_sem.at[0]),
        pltpu.make_async_copy(weight_ref, weight, in_sem.at[1]),
    ]
    for copy in load:
        copy.start()

    barrier = pltpu.get_barrier_semaphore()

    def greet(target):
        pl.semaphore_signal(barrier, inc=1, device_id=target, device_id_type=MESH)

    for target in (opposite, partner, sibling, *along_y, *along_z):
        greet(target)
    for block in range(2):
        for part_y in range(4):
            greet(device(h, l, part_y, 2 * y + block, d))

    for copy in load:
        copy.wait()
    root = jnp.sqrt(weight[...])
    own[...] = (raw[...].astype(jnp.float32) * root[None, :]).astype(jnp.bfloat16)

    @pl.when(outer)
    def _():
        at = pl.ds(pl.multiple_of(l * SNAP, SNAP), SNAP), pl.ds(pl.multiple_of(y * CELL, CELL), CELL)
        cols[at] = own[...]

    pl.semaphore_wait(barrier, 15)

    def remote(src, dst, send, recv, target):
        return pltpu.make_async_remote_copy(
            src_ref=src, dst_ref=dst, send_sem=send, recv_sem=recv, device_id=target, device_id_type=MESH
        )

    def sub_at(slot, sub):
        return rows.at[pl.ds(slot * PIECE + (sub // 4) * PART, PART), pl.ds((sub % 4) * CELL, CELL)]

    def chunk_at(which, chunk, cell_y):
        at = pl.multiple_of(which * SNAP + chunk * CHUNK, CHUNK)
        return cols.at[pl.ds(at, CHUNK), pl.ds(pl.multiple_of(cell_y * CELL, CELL), CELL)]

    def x_opposite(chunk, to_relay):
        src = own.at[pl.ds(chunk * CHUNK, CHUNK), :]
        if to_relay:
            return remote(src, relay.at[pl.ds(chunk * CHUNK, CHUNK), :], x_send.at[0, chunk], r_recv.at[chunk], opposite)
        return remote(src, chunk_at(l, chunk, y), x_send.at[0, chunk], x_recv.at[0, chunk], opposite)

    def x_partner(chunk, from_relay):
        if from_relay:
            src, which, first = relay.at[pl.ds(chunk * CHUNK, CHUNK), :], 1 - l, 1
        else:
            src, which, first = own.at[pl.ds(chunk * CHUNK, CHUNK), :], l, 0
        return remote(src, chunk_at(which, chunk, y), x_send.at[1, chunk], x_recv.at[first, chunk], partner)

    def x_start(chunk):
        @pl.when(outer)
        def _():
            x_opposite(chunk, True).start()

        @pl.when(inner)
        def _():
            x_opposite(chunk, False).start()
            x_partner(chunk, False).start()

    def x_relay(chunk):
        @pl.when(outer)
        def _():
            x_opposite(chunk, True).wait_recv()
            x_partner(chunk, True).start()

    half = lax.rem(z, 2)
    ring_y = z // 2
    a_index = half * 4 + y

    def a_copy(p, to_self):
        lanes = pl.ds(pl.multiple_of(y * CELL, CELL), CELL)
        src = cols.at[pl.ds(pl.multiple_of(h * SNAP + p * PART, PART), PART), lanes]
        dst = rows.at[pl.ds(pl.multiple_of(half * PART, PART), PART), lanes]
        if to_self:
            return pltpu.make_async_copy(src, dst, a_recv.at[a_index])
        return remote(src, dst, a_send.at[p], a_recv.at[a_index], device(h, l, ring_y, p, d))

    def a_start(chunk):
        for p in range(chunk * CHUNK // PART, (chunk + 1) * CHUNK // PART):

            @pl.when((y == ring_y) & (z == p))
            def _():
                a_copy(p, True).start()

            @pl.when((y != ring_y) | (z != p))
            def _():
                a_copy(p, False).start()

    def block_of(turn_of):
        return 1 - l if turn_of == 0 else l

    def y_copy(way, first, chunk):
        at = chunk_at(block_of(first), chunk, y)
        return remote(at, at, y_send.at[way, first, chunk], y_recv.at[way, first, chunk], along_y[way])

    def y_arrival(way, first, chunk):
        at = chunk_at(block_of(first), chunk, turn(y, (-1, 1)[way], 4))
        return remote(at, at, y_send.at[way, first, chunk], y_recv.at[way, first, chunk], along_y[way])

    def way_of(chunk):
        return chunk % 2

    def forward(first, chunk):
        way = way_of(chunk)
        y_arrival(way, first, chunk).wait_recv()
        forward_copy(first, chunk).start()

    def forward_copy(first, chunk):
        way = way_of(chunk)
        at = chunk_at(block_of(first), chunk, turn(y, (-1, 1)[way], 4))
        return remote(at, at, f_send.at[first, chunk], f_recv.at[first, chunk], along_y[way])

    def forward_arrival(first, chunk):
        at = chunk_at(block_of(first), chunk, turn(y, 2, 4))
        return remote(at, at, f_send.at[first, chunk], f_recv.at[first, chunk], along_y[way_of(chunk)])

    def x_wait(first, chunk):
        at = chunk_at(block_of(first), chunk, y)
        remote(at, at, x_send.at[0, chunk], x_recv.at[first, chunk], partner).wait_recv()

    def y_start(first, chunk):
        for way in (way_of(chunk), 1 - way_of(chunk)):
            y_copy(way, first, chunk).start()

    def y_finish(first):
        for chunk in range(CHUNKS):
            y_arrival(1 - way_of(chunk), first, chunk).wait_recv()
            forward_arrival(first, chunk).wait_recv()

    def slot_of(way, hop):
        return {0: 0, 4: 1}.get(hop, 2 * hop + way)

    def z_copy(way, hop, sub):
        return remote(
            sub_at(slot_of(way, hop), sub), sub_at(slot_of(way, hop + 1), sub),
            z_send.at[way, hop, sub], z_recv.at[way, hop, sub], along_z[way],
        )

    def z_wait(way, hop, sub):
        at = sub_at(slot_of(way, hop), sub)
        remote(at, at, z_send.at[way, hop - 1, sub], z_recv.at[way, hop - 1, sub], along_z[way]).wait_recv()

    def z_step(hop, sub):
        for way in range(2):
            z_wait(way, hop, sub)
            if hop < 3 or sub // 4 == way:
                z_copy(way, hop, sub).start()

    def rows_of(group):
        return pl.ds(group[0] * PIECE, group[1] * PIECE)

    def peer_copy(group, first):
        which, g = block_of(first), GROUPS.index(group)
        return remote(
            partial.at[1 - d, which, rows_of(group)], peer.at[which, rows_of(group)],
            p_send.at[first, g], p_recv.at[first, g], sibling,
        )

    def half_copy(group):
        g = GROUPS.index(group)
        return remote(
            half_out.at[rows_of(group)], half_in.at[rows_of(group)], q_send.at[g], q_recv.at[g], partner
        )

    def multiply(group, first):
        left = rows[rows_of(group), :]
        which = block_of(first)
        for side in range(2):
            at = pl.multiple_of(which * SNAP + side * COLS, COLS)
            partial[side, which, rows_of(group)] = lax.dot_general(
                left, cols[pl.ds(at, COLS), :], (((1,), (1,)), ((), ())), preferred_element_type=jnp.float32
            )
        peer_copy(group, first).start()

    def sum_cores(group):
        peer_copy(group, 0).wait_recv()
        at = rows_of(group)
        half_out[at] = (partial[d, 1 - l, at] + peer[1 - l, at]).astype(jnp.bfloat16)
        half_copy(group).start()

    def sum_chips(group):
        peer_copy(group, 1).wait_recv()
        half_copy(group).wait_recv()
        at = rows_of(group)
        total = partial[d, l, at] + peer[l, at] + half_in[at].astype(jnp.float32)
        total = total * jnp.float32(1.0 / CELLS)
        for i in range(group[1]):
            off = {OWN: 0, OPPOSITE: 4}.get(group, (-1, 1)[i] * (group[0] // 2))
            to = pl.multiple_of(turn(z, off, 8) * PART, PART)
            out_ref[pl.ds(to, PART), :] = total[i * PIECE : i * PIECE + PART]
            out_ref[pl.ds(SNAP + to, PART), :] = total[i * PIECE + PART : (i + 1) * PIECE]

    def z_first(sub):
        at = sub_at(0, sub)
        remote(at, at, a_send.at[0], a_recv.at[sub], partner).wait_recv()
        for way in range(2):
            z_copy(way, 0, sub).start()

    for i in range(CHUNKS):
        x_start(i)

        @pl.when(outer)
        def _():
            a_start(i)

    for i in range(CHUNKS):
        x_relay(i)
        x_wait(0, i)

        @pl.when(inner)
        def _():
            a_start(i)

        y_start(0, i)
    for i in range(CHUNKS):

        @pl.when(inner)
        def _():
            x_wait(1, i)

        y_start(1, i)
        forward(0, i)
        z_first(2 * i)
        z_first(2 * i + 1)
    for sub in range(8):
        z_step(1, sub)
        if sub >= 6:
            forward(1, sub - 6)
    y_finish(0)
    multiply(OWN, 0)
    multiply(HOP1, 0)
    for sub in range(8):
        z_step(2, sub)
        if sub in (1, 3):
            forward(1, 2 + sub // 2)
        if sub == 3:
            sum_cores(OWN)
            sum_cores(HOP1)
    multiply(HOP2, 0)
    for sub in range(8):
        z_step(3, sub)
        if sub == 3:
            sum_cores(HOP2)
    multiply(HOP3, 0)
    y_finish(1)
    multiply(OWN, 1)
    multiply(HOP1, 1)
    sum_cores(HOP3)
    multiply(HOP2, 1)
    sum_chips(OWN)
    multiply(HOP3, 1)
    for sub in range(8):
        z_wait(sub // 4, 4, sub)
    multiply(OPPOSITE, 0)
    multiply(OPPOSITE, 1)
    sum_cores(OPPOSITE)
    sum_chips(HOP1)
    sum_chips(HOP2)
    sum_chips(HOP3)
    sum_chips(OPPOSITE)

    for p in range(8):

        @pl.when((y != ring_y) | (z != p))
        def _():
            a_copy(p, False).wait_send()

    for chunk in range(CHUNKS):
        x_opposite(chunk, True).wait_send()
        x_partner(chunk, True).wait_send()
    for first in range(2):
        for chunk in range(CHUNKS):
            for way in range(2):
                y_copy(way, first, chunk).wait_send()
            forward_copy(first, chunk).wait_send()
    for way in range(2):
        for hop in range(4):
            for sub in range(8):
                if hop < 3 or sub // 4 == way:
                    z_copy(way, hop, sub).wait_send()
    for group in GROUPS:
        for first in range(2):
            peer_copy(group, first).wait_send()
        half_copy(group).wait_send()


def on_device(snapshots, cell_weight):
    hbm = pl.BlockSpec(memory_space=pltpu.HBM)
    dma = pltpu.SemaphoreType.DMA
    return pl.pallas_call(
        kernel,
        out_shape=jax.ShapeDtypeStruct((2 * SNAP, COLS), jnp.float32),
        in_specs=[hbm, hbm],
        out_specs=pl.BlockSpec(memory_space=pltpu.VMEM),
        scratch_shapes=[
            pltpu.VMEM((SNAP, CELL), jnp.bfloat16),
            pltpu.VMEM((CELL,), jnp.float32),
            pltpu.VMEM((SNAP, CELL), jnp.bfloat16),
            pltpu.VMEM((SNAP, CELL), jnp.bfloat16),
            pltpu.VMEM((2 * SNAP, 4 * CELL), jnp.bfloat16),
            pltpu.VMEM((8 * PIECE, 4 * CELL), jnp.bfloat16),
            pltpu.VMEM((2, 2, 8 * PIECE, COLS), jnp.float32),
            pltpu.VMEM((2, 8 * PIECE, COLS), jnp.float32),
            pltpu.VMEM((8 * PIECE, COLS), jnp.bfloat16),
            pltpu.VMEM((8 * PIECE, COLS), jnp.bfloat16),
            dma((2,)),
            dma((8,)), dma((8,)),
            dma((CHUNKS,)), dma((2, CHUNKS)), dma((2, CHUNKS)),
            dma((2, 2, CHUNKS)), dma((2, 2, CHUNKS)),
            dma((2, CHUNKS)), dma((2, CHUNKS)),
            dma((2, 4, 8)), dma((2, 4, 8)),
            dma((2, 5)), dma((2, 5)), dma((5,)), dma((5,)),
        ],
        compiler_params=pltpu.CompilerParams(
            collective_id=0, has_side_effects=True, vmem_limit_bytes=60 << 20
        ),
        name="gram",
    )(snapshots, cell_weight)


def solution(mesh):
    return jax.shard_map(
        on_device,
        mesh=mesh,
        in_specs=(P("col", ("row", "depth")), P(("row", "depth"))),
        out_specs=P("row", ("col", "depth")),
        check_vma=False,
    )
```

time: 313 us -> 71.6 us (0.23)
  waiting for transfers between devices: 274 us -> 0 us
  Pallas kernels: 0 us -> 69.2 us
  between operations: 13.2 us -> 0.01 us
  matrix products: 10.1 us -> 0 us
  other arithmetic: 7.09 us -> 0 us
  blocking collectives: 6.92 us -> 0 us
    psum x1 -> x0, waiting for transfers between devices: 162 us -> none  [spread(): return lax.psum(jnp.where(mine, value, jnp.zeros_like(value)), axis)]
    all_gather x3 -> x0, waiting for transfers between devices: 111 us -> none  [the longest x1 68.3 us: on_device(): column_rows = lax.all_gather(own_half, 'row', axis=1, tiled=True)]
    pallas_call x0 -> x1, Pallas kernels: none -> 69.2 us  [on_device(): pl.pallas_call(kernel, out_shape=jax.ShapeDtypeStruct((2 * SNAP, COLS), j...]
    dot_general x2 -> x0, matrix products: 10.1 us -> none  [block_product(): lax.dot_general(left_rows, right_rows, (((1,), (1,)), ((), ())), preferre...]
    all_to_all x1 -> x0, blocking collectives: 6.92 us -> none  [on_device(): lax.all_to_all(scaled, 'depth', split_axis=0, concat_axis=1, tiled=True)]
    select_n x1 -> x0, other arithmetic: 4.94 us -> none  [spread(): return lax.psum(jnp.where(mine, value, jnp.zeros_like(value)), axis)]
  transfers between devices with their start and end apart: 4 -> 0, of which waited for: 4 -> 0; matrix products, arithmetic and copies ran while one was open for 2% -> 0% of each run, Pallas kernels for 0% -> 0%
where the time goes in v2:
time: 71.6 us; the launch traced here: 71.4 us
  Pallas kernels  69.2 us (97%)
  local copies, waits for them, and re-layouts  2.26 us (3%)
    pallas_call x1, Pallas kernels, on_device(): pl.pallas_call(kernel, out_shape=jax.ShapeDtypeStruct((2 * SNAP, COLS), j...  69.2 us
    unnamed x1, local copies, waits for them, and re-layouts  2.26 us

profile of v2, /device:TPU:1, one launch (start us, length us, event | category | flops | bytes accessed | tf_op | source)
XLA Modules:
  0.0 71.4 jit_solution(18092758969976126873)
XLA Ops:
  0.0 69.2 %gram.1 = f32[1024,256]{1,0:T(8,128)} custom-call(bf16[512,384]{1,0:T(8,128)(2,1)} %snap_ref.1, f32[384]{0:T(512)} %weight_ref.1), custom_call_target="tpu_custom_call" | custom-call | tf_op jit(solution)/shard_map/gram/pallas_call | solution.py:339
  69.2 2.3 %copy.4 = f32[1024,256]{1,0:T(8,128)} copy(f32[1024,256]{1,0:T(8,128)} %gram.1) | data formatting | bytes 2097152

commit v3 on v2

--- a/solution.py
+++ b/solution.py
@@ -57,7 +57,7 @@
         greet(target)
     for block in range(2):
         for part_y in range(4):
-            greet(device(h, l, part_y, 2 * y + block, d))
+            greet(device(l, h, part_y, 2 * y + block, d))
 
     for copy in load:
         copy.wait()
@@ -116,24 +116,24 @@
     ring_y = z // 2
     a_index = half * 4 + y
 
+    def stays(p):
+        return outer & (y == ring_y) & (z == p)
+
     def a_copy(p, to_self):
-        lanes = pl.ds(pl.multiple_of(y * CELL, CELL), CELL)
-        src = cols.at[pl.ds(pl.multiple_of(h * SNAP + p * PART, PART), PART), lanes]
-        dst = rows.at[pl.ds(pl.multiple_of(half * PART, PART), PART), lanes]
+        src = own.at[pl.ds(p * PART, PART), :]
+        dst = rows.at[pl.ds(pl.multiple_of(half * PART, PART), PART), pl.ds(pl.multiple_of(y * CELL, CELL), CELL)]
         if to_self:
             return pltpu.make_async_copy(src, dst, a_recv.at[a_index])
-        return remote(src, dst, a_send.at[p], a_recv.at[a_index], device(h, l, ring_y, p, d))
-
-    def a_start(chunk):
-        for p in range(chunk * CHUNK // PART, (chunk + 1) * CHUNK // PART):
-
-            @pl.when((y == ring_y) & (z == p))
-            def _():
-                a_copy(p, True).start()
-
-            @pl.when((y != ring_y) | (z != p))
-            def _():
-                a_copy(p, False).start()
+        return remote(src, dst, a_send.at[p], a_recv.at[a_index], device(l, h, ring_y, p, d))
+
+    def a_start(p):
+        @pl.when(stays(p))
+        def _():
+            a_copy(p, True).start()
+
+        @pl.when(jnp.logical_not(stays(p)))
+        def _():
+            a_copy(p, False).start()
 
     def block_of(turn_of):
         return 1 - l if turn_of == 0 else l
@@ -245,51 +245,50 @@
         for way in range(2):
             z_copy(way, 0, sub).start()
 
+    def y_second(chunk):
+        @pl.when(inner)
+        def _():
+            x_wait(1, chunk)
+
+        y_start(1, chunk)
+
+    def y_first(chunk):
+        x_wait(0, chunk)
+        y_start(0, chunk)
+
+    for p in range(8):
+        a_start(p)
     for i in range(CHUNKS):
         x_start(i)
-
-        @pl.when(outer)
-        def _():
-            a_start(i)
-
     for i in range(CHUNKS):
         x_relay(i)
-        x_wait(0, i)
-
-        @pl.when(inner)
-        def _():
-            a_start(i)
-
-        y_start(0, i)
-    for i in range(CHUNKS):
-
-        @pl.when(inner)
-        def _():
-            x_wait(1, i)
-
-        y_start(1, i)
-        forward(0, i)
-        z_first(2 * i)
-        z_first(2 * i + 1)
+        if i >= 2:
+            y_second(i - 2)
+    for sub in range(8):
+        z_first(sub)
     for sub in range(8):
         z_step(1, sub)
-        if sub >= 6:
-            forward(1, sub - 6)
+        if sub % 2 == 1:
+            y_first(sub // 2)
+    for sub in range(8):
+        z_step(2, sub)
+        if sub in (0, 1, 2, 4):
+            forward(0, (0, 1, 2, None, 3)[sub])
+        if sub == 1:
+            y_second(2)
+            y_second(3)
     y_finish(0)
     multiply(OWN, 0)
     multiply(HOP1, 0)
     for sub in range(8):
-        z_step(2, sub)
-        if sub in (1, 3):
-            forward(1, 2 + sub // 2)
+        z_step(3, sub)
+        if sub < 4:
+            forward(1, sub)
         if sub == 3:
             sum_cores(OWN)
             sum_cores(HOP1)
     multiply(HOP2, 0)
-    for sub in range(8):
-        z_step(3, sub)
-        if sub == 3:
-            sum_cores(HOP2)
+    sum_cores(HOP2)
     multiply(HOP3, 0)
     y_finish(1)
     multiply(OWN, 1)
@@ -310,7 +309,7 @@
 
     for p in range(8):
 
-        @pl.when((y != ring_y) | (z != p))
+        @pl.when(jnp.logical_not(stays(p)))
         def _():
             a_copy(p, False).wait_send()
 
@@ -361,10 +360,10 @@
             dma((2, 5)), dma((2, 5)), dma((5,)), dma((5,)),
         ],
         compiler_params=pltpu.CompilerParams(
-            collective_id=0, has_side_effects=True, vmem_limit_bytes=60 << 20
+            collective_id=0, has_side_effects=True, vmem_limit_bytes=40 << 20
         ),
         name="gram",
-    )(snapshots, cell_weight)
+    )(pltpu.with_memory_space_constraint(snapshots, pltpu.HBM), pltpu.with_memory_space_constraint(cell_weight, pltpu.HBM))
 
 
 def solution(mesh):

time: 71.6 us -> 65 us (0.908)
  Pallas kernels: 69.2 us -> 63.9 us
  local copies, waits for them, and re-layouts: 2.26 us -> 0.97 us
    pallas_call x1, Pallas kernels: 69.2 us -> 63.9 us  [on_device(): pl.pallas_call(kernel, out_shape=jax.ShapeDtypeStruct((2 * SNAP, COLS), j...]
    unnamed x1, local copies, waits for them, and re-layouts: 2.26 us -> 0.97 us
where the time goes in v3:
time: 65 us; the launch traced here: 64.9 us
  Pallas kernels  63.9 us (98%)
  local copies, waits for them, and re-layouts  0.97 us (1%)
    pallas_call x1, Pallas kernels, on_device(): pl.pallas_call(kernel, out_shape=jax.ShapeDtypeStruct((2 * SNAP, COLS), j...  63.9 us

profile of v3, /device:TPU:1, one launch (start us, length us, event | category | flops | bytes accessed | tf_op | source)
XLA Modules:
  0.0 64.9 jit_solution(11366824973843105476)
XLA Ops:
  0.0 63.9 %gram.1 = f32[1024,256]{1,0:T(8,128)S(1)} custom-call(bf16[512,384]{1,0:T(8,128)(2,1)} %snap_ref.1, f32[384]{0:T(512)} %weight_ref.1), custom_call_target="tpu_custom_call" | custom-call | tf_op jit(solution)/shard_map/gram/pallas_call | solution.py:338
  63.9 1.0 %copy.4 = f32[1024,256]{1,0:T(8,128)} copy(f32[1024,256]{1,0:T(8,128)S(1)} %gram.1) | data formatting | bytes 2097152

commit v4 on v3

--- a/solution.py
+++ b/solution.py
@@ -14,9 +14,11 @@
 COLS = 256
 CHUNK = 128
 CHUNKS = SNAP // CHUNK
-
-OWN, OPPOSITE, HOP1, HOP2, HOP3 = (0, 1), (1, 1), (2, 2), (4, 2), (6, 2)
-GROUPS = (OWN, HOP1, HOP2, HOP3, OPPOSITE)
+STRIP = 16
+
+OWN, HOP1, HOP2, HOP3 = (0, PIECE), (2 * PIECE, 2 * PIECE), (4 * PIECE, 2 * PIECE), (6 * PIECE, 2 * PIECE)
+LAST = (PIECE, PIECE)
+GROUPS = (OWN, HOP1, HOP2, HOP3, LAST)
 
 
 def kernel(
@@ -77,7 +79,7 @@
         )
 
     def sub_at(slot, sub):
-        return rows.at[pl.ds(slot * PIECE + (sub // 4) * PART, PART), pl.ds((sub % 4) * CELL, CELL)]
+        return rows.at[pl.ds(slot * PIECE + sub * STRIP, STRIP), :]
 
     def chunk_at(which, chunk, cell_y):
         at = pl.multiple_of(which * SNAP + chunk * CHUNK, CHUNK)
@@ -96,16 +98,6 @@
             src, which, first = own.at[pl.ds(chunk * CHUNK, CHUNK), :], l, 0
         return remote(src, chunk_at(which, chunk, y), x_send.at[1, chunk], x_recv.at[first, chunk], partner)
 
-    def x_start(chunk):
-        @pl.when(outer)
-        def _():
-            x_opposite(chunk, True).start()
-
-        @pl.when(inner)
-        def _():
-            x_opposite(chunk, False).start()
-            x_partner(chunk, False).start()
-
     def x_relay(chunk):
         @pl.when(outer)
         def _():
@@ -119,21 +111,32 @@
     def stays(p):
         return outer & (y == ring_y) & (z == p)
 
-    def a_copy(p, to_self):
-        src = own.at[pl.ds(p * PART, PART), :]
-        dst = rows.at[pl.ds(pl.multiple_of(half * PART, PART), PART), pl.ds(pl.multiple_of(y * CELL, CELL), CELL)]
+    def a_copy(chunk, p, to_self):
+        src = own.at[pl.ds(chunk * CHUNK + p * STRIP, STRIP), :]
+        dst = rows.at[
+            pl.ds(pl.multiple_of((2 * chunk + half) * STRIP, STRIP), STRIP),
+            pl.ds(pl.multiple_of(y * CELL, CELL), CELL),
+        ]
+        recv = a_recv.at[chunk, a_index]
         if to_self:
-            return pltpu.make_async_copy(src, dst, a_recv.at[a_index])
-        return remote(src, dst, a_send.at[p], a_recv.at[a_index], device(l, h, ring_y, p, d))
-
-    def a_start(p):
-        @pl.when(stays(p))
-        def _():
-            a_copy(p, True).start()
-
-        @pl.when(jnp.logical_not(stays(p)))
-        def _():
-            a_copy(p, False).start()
+            return pltpu.make_async_copy(src, dst, recv)
+        return remote(src, dst, a_send.at[chunk, p], recv, device(l, h, ring_y, p, d))
+
+    def a_start(chunk):
+        for p in range(8):
+
+            @pl.when(stays(p))
+            def _():
+                a_copy(chunk, p, True).start()
+
+            @pl.when(jnp.logical_not(stays(p)))
+            def _():
+                a_copy(chunk, p, False).start()
+
+    def a_wait(chunk, block):
+        for cell_y in range(4):
+            at = rows.at[pl.ds((2 * chunk + block) * STRIP, STRIP), pl.ds(cell_y * CELL, CELL)]
+            remote(at, at, a_send.at[0, 0], a_recv.at[chunk, block * 4 + cell_y], partner).wait_recv()
 
     def block_of(turn_of):
         return 1 - l if turn_of == 0 else l
@@ -171,8 +174,8 @@
         for way in (way_of(chunk), 1 - way_of(chunk)):
             y_copy(way, first, chunk).start()
 
-    def y_finish(first):
-        for chunk in range(CHUNKS):
+    def y_finish(first, side):
+        for chunk in (2 * side, 2 * side + 1):
             y_arrival(1 - way_of(chunk), first, chunk).wait_recv()
             forward_arrival(first, chunk).wait_recv()
 
@@ -192,11 +195,11 @@
     def z_step(hop, sub):
         for way in range(2):
             z_wait(way, hop, sub)
-            if hop < 3 or sub // 4 == way:
+            if hop < 3 or sub % 2 == way:
                 z_copy(way, hop, sub).start()
 
     def rows_of(group):
-        return pl.ds(group[0] * PIECE, group[1] * PIECE)
+        return pl.ds(*group)
 
     def peer_copy(group, first):
         which, g = block_of(first), GROUPS.index(group)
@@ -211,15 +214,21 @@
             half_out.at[rows_of(group)], half_in.at[rows_of(group)], q_send.at[g], q_recv.at[g], partner
         )
 
+    def multiply_side(group, first, side):
+        which = block_of(first)
+        at = pl.multiple_of(which * SNAP + side * COLS, COLS)
+        partial[side, which, rows_of(group)] = lax.dot_general(
+            rows[rows_of(group), :], cols[pl.ds(at, COLS), :], (((1,), (1,)), ((), ())),
+            preferred_element_type=jnp.float32,
+        )
+
+        @pl.when(d != side)
+        def _():
+            peer_copy(group, first).start()
+
     def multiply(group, first):
-        left = rows[rows_of(group), :]
-        which = block_of(first)
         for side in range(2):
-            at = pl.multiple_of(which * SNAP + side * COLS, COLS)
-            partial[side, which, rows_of(group)] = lax.dot_general(
-                left, cols[pl.ds(at, COLS), :], (((1,), (1,)), ((), ())), preferred_element_type=jnp.float32
-            )
-        peer_copy(group, first).start()
+            multiply_side(group, first, side)
 
     def sum_cores(group):
         peer_copy(group, 0).wait_recv()
@@ -233,17 +242,17 @@
         at = rows_of(group)
         total = partial[d, l, at] + peer[l, at] + half_in[at].astype(jnp.float32)
         total = total * jnp.float32(1.0 / CELLS)
-        for i in range(group[1]):
-            off = {OWN: 0, OPPOSITE: 4}.get(group, (-1, 1)[i] * (group[0] // 2))
-            to = pl.multiple_of(turn(z, off, 8) * PART, PART)
-            out_ref[pl.ds(to, PART), :] = total[i * PIECE : i * PIECE + PART]
-            out_ref[pl.ds(SNAP + to, PART), :] = total[i * PIECE + PART : (i + 1) * PIECE]
-
-    def z_first(sub):
-        at = sub_at(0, sub)
-        remote(at, at, a_send.at[0], a_recv.at[sub], partner).wait_recv()
-        for way in range(2):
-            z_copy(way, 0, sub).start()
+        for i in range(group[1] // STRIP):
+            slot, sub = divmod(group[0] // STRIP + i, PIECE // STRIP)
+            off = {0: 0, 1: 4}.get(slot, (-1, 1)[slot % 2] * (slot // 2))
+            to = (sub % 2) * SNAP + (sub // 2) * CHUNK + turn(z, off, 8) * STRIP
+            out_ref[pl.ds(pl.multiple_of(to, STRIP), STRIP), :] = total[i * STRIP : (i + 1) * STRIP]
+
+    def z_first(chunk):
+        for block in range(2):
+            a_wait(chunk, block)
+            for way in range(2):
+                z_copy(way, 0, chunk * 2 + block).start()
 
     def y_second(chunk):
         @pl.when(inner)
@@ -256,62 +265,77 @@
         x_wait(0, chunk)
         y_start(0, chunk)
 
-    for p in range(8):
-        a_start(p)
-    for i in range(CHUNKS):
-        x_start(i)
-    for i in range(CHUNKS):
-        x_relay(i)
-        if i >= 2:
-            y_second(i - 2)
+    @pl.when(outer)
+    def _():
+        for chunk in range(CHUNKS):
+            x_opposite(chunk, True).start()
+
+    for chunk in range(CHUNKS):
+        a_start(chunk)
+
+    @pl.when(inner)
+    def _():
+        for chunk in range(CHUNKS):
+            x_partner(chunk, False).start()
+            x_opposite(chunk, False).start()
+
+    for chunk in range(CHUNKS):
+        z_first(chunk)
+        x_relay(chunk)
+        if chunk >= 2:
+            y_second(chunk - 2)
+    after = {
+        (1, 1): [lambda: y_first(0)],
+        (1, 3): [lambda: y_first(1)],
+        (1, 5): [lambda: y_first(2)],
+        (1, 7): [lambda: y_first(3)],
+        (2, 0): [lambda: forward(0, 0)],
+        (2, 1): [lambda: forward(0, 1)],
+        (2, 2): [lambda: y_second(2), lambda: y_second(3)],
+        (2, 3): [lambda: forward(0, 2), lambda: forward(1, 0)],
+        (2, 4): [lambda: forward(0, 3)],
+        (2, 5): [lambda: forward(1, 1)],
+        (2, 7): [lambda: y_finish(0, 0), lambda: multiply_side(OWN, 0, 0)],
+        (3, 0): [lambda: multiply_side(HOP1, 0, 0), lambda: y_finish(0, 1)],
+        (3, 1): [lambda: multiply_side(OWN, 0, 1), lambda: forward(1, 2)],
+        (3, 2): [lambda: multiply_side(HOP1, 0, 1), lambda: forward(1, 3)],
+        (3, 3): [lambda: multiply_side(HOP2, 0, 0), lambda: sum_cores(OWN)],
+        (3, 4): [lambda: multiply_side(HOP2, 0, 1), lambda: sum_cores(HOP1)],
+        (3, 5): [lambda: y_finish(1, 0), lambda: multiply_side(OWN, 1, 0)],
+        (3, 6): [lambda: multiply_side(HOP1, 1, 0)],
+        (3, 7): [lambda: multiply_side(HOP2, 1, 0)],
+    }
+    for hop in range(1, 4):
+        for sub in range(8):
+            z_step(hop, sub)
+            for action in after.get((hop, sub), ()):
+                action()
+    multiply(HOP3, 0)
+    sum_cores(HOP2)
+    multiply_side(HOP3, 1, 0)
+    y_finish(1, 1)
+    multiply_side(OWN, 1, 1)
+    sum_cores(HOP3)
+    for group in (HOP1, HOP2, HOP3):
+        multiply_side(group, 1, 1)
+    sum_chips(OWN)
+    sum_chips(HOP1)
     for sub in range(8):
-        z_first(sub)
-    for sub in range(8):
-        z_step(1, sub)
-        if sub % 2 == 1:
-            y_first(sub // 2)
-    for sub in range(8):
-        z_step(2, sub)
-        if sub in (0, 1, 2, 4):
-            forward(0, (0, 1, 2, None, 3)[sub])
-        if sub == 1:
-            y_second(2)
-            y_second(3)
-    y_finish(0)
-    multiply(OWN, 0)
-    multiply(HOP1, 0)
-    for sub in range(8):
-        z_step(3, sub)
-        if sub < 4:
-            forward(1, sub)
-        if sub == 3:
-            sum_cores(OWN)
-            sum_cores(HOP1)
-    multiply(HOP2, 0)
-    sum_cores(HOP2)
-    multiply(HOP3, 0)
-    y_finish(1)
-    multiply(OWN, 1)
-    multiply(HOP1, 1)
-    sum_cores(HOP3)
-    multiply(HOP2, 1)
-    sum_chips(OWN)
-    multiply(HOP3, 1)
-    for sub in range(8):
-        z_wait(sub // 4, 4, sub)
-    multiply(OPPOSITE, 0)
-    multiply(OPPOSITE, 1)
-    sum_cores(OPPOSITE)
-    sum_chips(HOP1)
+        z_wait(sub % 2, 4, sub)
+    multiply(LAST, 0)
+    multiply_side(LAST, 1, 0)
+    sum_cores(LAST)
+    multiply_side(LAST, 1, 1)
     sum_chips(HOP2)
     sum_chips(HOP3)
-    sum_chips(OPPOSITE)
+    sum_chips(LAST)
 
     for p in range(8):
 
         @pl.when(jnp.logical_not(stays(p)))
         def _():
-            a_copy(p, False).wait_send()
+            for chunk in range(CHUNKS):
+                a_copy(chunk, p, False).wait_send()
 
     for chunk in range(CHUNKS):
         x_opposite(chunk, True).wait_send()
@@ -324,7 +348,7 @@
     for way in range(2):
         for hop in range(4):
             for sub in range(8):
-                if hop < 3 or sub // 4 == way:
+                if hop < 3 or sub % 2 == way:
                     z_copy(way, hop, sub).wait_send()
     for group in GROUPS:
         for first in range(2):
@@ -352,12 +376,12 @@
             pltpu.VMEM((8 * PIECE, COLS), jnp.bfloat16),
             pltpu.VMEM((8 * PIECE, COLS), jnp.bfloat16),
             dma((2,)),
-            dma((8,)), dma((8,)),
+            dma((CHUNKS, 8)), dma((CHUNKS, 8)),
             dma((CHUNKS,)), dma((2, CHUNKS)), dma((2, CHUNKS)),
             dma((2, 2, CHUNKS)), dma((2, 2, CHUNKS)),
             dma((2, CHUNKS)), dma((2, CHUNKS)),
             dma((2, 4, 8)), dma((2, 4, 8)),
-            dma((2, 5)), dma((2, 5)), dma((5,)), dma((5,)),
+            dma((2, 6)), dma((2, 6)), dma((6,)), dma((6,)),
         ],
         compiler_params=pltpu.CompilerParams(
             collective_id=0, has_side_effects=True, vmem_limit_bytes=40 << 20

time: 65 us -> 63.4 us (0.975)
  Pallas kernels: 63.9 us -> 62.3 us
    pallas_call x1, Pallas kernels: 63.9 us -> 62.3 us  [on_device(): pl.pallas_call(kernel, out_shape=jax.ShapeDtypeStruct((2 * SNAP, COLS), j...]
where the time goes in v4:
time: 63.4 us; the launch traced here: 63.3 us
  Pallas kernels  62.3 us (98%)
  local copies, waits for them, and re-layouts  0.97 us (2%)
    pallas_call x1, Pallas kernels, on_device(): pl.pallas_call(kernel, out_shape=jax.ShapeDtypeStruct((2 * SNAP, COLS), j...  62.3 us

profile of v4, /device:TPU:1, one launch (start us, length us, event | category | flops | bytes accessed | tf_op | source)
XLA Modules:
  0.0 63.3 jit_solution(15665604651404823421)
XLA Ops:
  0.0 62.3 %gram.1 = f32[1024,256]{1,0:T(8,128)S(1)} custom-call(bf16[512,384]{1,0:T(8,128)(2,1)} %snap_ref.1, f32[384]{0:T(512)} %weight_ref.1), custom_call_target="tpu_custom_call" | custom-call | tf_op jit(solution)/shard_map/gram/pallas_call | solution.py:362
  62.3 1.0 %copy.4 = f32[1024,256]{1,0:T(8,128)} copy(f32[1024,256]{1,0:T(8,128)S(1)} %gram.1) | data formatting | bytes 2097152

commit v5 on v4

--- a/solution.py
+++ b/solution.py
@@ -15,6 +15,7 @@
 CHUNK = 128
 CHUNKS = SNAP // CHUNK
 STRIP = 16
+SUBS = ((0, 1, 2, 3, 4, 5, 6, 7), (4, 5, 6, 7, 0, 1, 2, 3))
 
 OWN, HOP1, HOP2, HOP3 = (0, PIECE), (2 * PIECE, 2 * PIECE), (4 * PIECE, 2 * PIECE), (6 * PIECE, 2 * PIECE)
 LAST = (PIECE, PIECE)
@@ -192,11 +193,11 @@
         at = sub_at(slot_of(way, hop), sub)
         remote(at, at, z_send.at[way, hop - 1, sub], z_recv.at[way, hop - 1, sub], along_z[way]).wait_recv()
 
-    def z_step(hop, sub):
+    def z_step(hop, k):
         for way in range(2):
-            z_wait(way, hop, sub)
-            if hop < 3 or sub % 2 == way:
-                z_copy(way, hop, sub).start()
+            z_wait(way, hop, SUBS[way][k])
+            if hop < 3 or k < 4:
+                z_copy(way, hop, SUBS[way][k]).start()
 
     def rows_of(group):
         return pl.ds(*group)
@@ -248,11 +249,9 @@
             to = (sub % 2) * SNAP + (sub // 2) * CHUNK + turn(z, off, 8) * STRIP
             out_ref[pl.ds(pl.multiple_of(to, STRIP), STRIP), :] = total[i * STRIP : (i + 1) * STRIP]
 
-    def z_first(chunk):
-        for block in range(2):
-            a_wait(chunk, block)
-            for way in range(2):
-                z_copy(way, 0, chunk * 2 + block).start()
+    def z_first(way, ks):
+        for k in ks:
+            z_copy(way, 0, SUBS[way][k]).start()
 
     def y_second(chunk):
         @pl.when(inner)
@@ -270,7 +269,7 @@
         for chunk in range(CHUNKS):
             x_opposite(chunk, True).start()
 
-    for chunk in range(CHUNKS):
+    for chunk in (0, 2, 1, 3):
         a_start(chunk)
 
     @pl.when(inner)
@@ -279,11 +278,16 @@
             x_partner(chunk, False).start()
             x_opposite(chunk, False).start()
 
-    for chunk in range(CHUNKS):
-        z_first(chunk)
-        x_relay(chunk)
-        if chunk >= 2:
-            y_second(chunk - 2)
+    for i, chunk in enumerate((0, 2, 1, 3)):
+        for block in range(2):
+            a_wait(chunk, block)
+        z_first(i % 2, (0, 1) if i < 2 else (2, 3))
+        x_relay(i)
+        if i >= 2:
+            y_second(i - 2)
+    for ks in ((4, 5), (6, 7)):
+        for way in range(2):
+            z_first(way, ks)
     after = {
         (1, 1): [lambda: y_first(0)],
         (1, 3): [lambda: y_first(1)],
@@ -300,10 +304,9 @@
         (3, 1): [lambda: multiply_side(OWN, 0, 1), lambda: forward(1, 2)],
         (3, 2): [lambda: multiply_side(HOP1, 0, 1), lambda: forward(1, 3)],
         (3, 3): [lambda: multiply_side(HOP2, 0, 0), lambda: sum_cores(OWN)],
-        (3, 4): [lambda: multiply_side(HOP2, 0, 1), lambda: sum_cores(HOP1)],
-        (3, 5): [lambda: y_finish(1, 0), lambda: multiply_side(OWN, 1, 0)],
-        (3, 6): [lambda: multiply_side(HOP1, 1, 0)],
-        (3, 7): [lambda: multiply_side(HOP2, 1, 0)],
+        (3, 4): [lambda: multiply_side(HOP2, 0, 1)],
+        (3, 5): [lambda: sum_cores(HOP1)],
+        (3, 6): [lambda: sum_cores(HOP2)],
     }
     for hop in range(1, 4):
         for sub in range(8):
@@ -311,25 +314,22 @@
             for action in after.get((hop, sub), ()):
                 action()
     multiply(HOP3, 0)
-    sum_cores(HOP2)
-    multiply_side(HOP3, 1, 0)
+    y_finish(1, 0)
+    multiply_side(OWN, 1, 0)
+    multiply_side(HOP1, 1, 0)
+    sum_cores(HOP3)
     y_finish(1, 1)
     multiply_side(OWN, 1, 1)
-    sum_cores(HOP3)
-    for group in (HOP1, HOP2, HOP3):
-        multiply_side(group, 1, 1)
-    sum_chips(OWN)
-    sum_chips(HOP1)
+    multiply_side(HOP1, 1, 1)
+    multiply(HOP2, 1)
     for sub in range(8):
-        z_wait(sub % 2, 4, sub)
+        z_wait(sub // 4, 4, sub)
     multiply(LAST, 0)
-    multiply_side(LAST, 1, 0)
+    multiply(HOP3, 1)
     sum_cores(LAST)
-    multiply_side(LAST, 1, 1)
-    sum_chips(HOP2)
-    sum_chips(HOP3)
-    sum_chips(LAST)
-
+    multiply(LAST, 1)
+    for group in GROUPS:
+        sum_chips(group)
     for p in range(8):
 
         @pl.when(jnp.logical_not(stays(p)))
@@ -348,7 +348,7 @@
     for way in range(2):
         for hop in range(4):
             for sub in range(8):
-                if hop < 3 or sub % 2 == way:
+                if hop < 3 or sub // 4 == way:
                     z_copy(way, hop, sub).wait_send()
     for group in GROUPS:
         for first in range(2):

time: 63.4 us -> 63.3 us (level)
  no operation moved by 1% of the time
where the time goes in v5:
time: 63.3 us; the launch traced here: 63 us
  Pallas kernels  62 us (98%)
  local copies, waits for them, and re-layouts  0.97 us (2%)
    pallas_call x1, Pallas kernels, on_device(): pl.pallas_call(kernel, out_shape=jax.ShapeDtypeStruct((2 * SNAP, COLS), j...  62 us

profile of v5, /device:TPU:1, one launch (start us, length us, event | category | flops | bytes accessed | tf_op | source)
XLA Modules:
  0.0 63.0 jit_solution(15531154424380627769)
XLA Ops:
  0.0 62.0 %gram.1 = f32[1024,256]{1,0:T(8,128)S(1)} custom-call(bf16[512,384]{1,0:T(8,128)(2,1)} %snap_ref.1, f32[384]{0:T(512)} %weight_ref.1), custom_call_target="tpu_custom_call" | custom-call | tf_op jit(solution)/shard_map/gram/pallas_call | solution.py:362
  62.0 1.0 %copy.4 = f32[1024,256]{1,0:T(8,128)} copy(f32[1024,256]{1,0:T(8,128)S(1)} %gram.1) | data formatting | bytes 2097152

commit v6 on v5

--- a/solution.py
+++ b/solution.py
@@ -226,6 +226,17 @@
         @pl.when(d != side)
         def _():
             peer_copy(group, first).start()
+
+    def multiply_urgent(group):
+        which = block_of(0)
+        for side in (1 - d, d):
+            at = pl.multiple_of(which * SNAP + side * COLS, COLS)
+            partial[side, which, rows_of(group)] = lax.dot_general(
+                rows[rows_of(group), :], cols[pl.ds(at, COLS), :], (((1,), (1,)), ((), ())),
+                preferred_element_type=jnp.float32,
+            )
+            if side is not d:
+                peer_copy(group, 0).start()
 
     def multiply(group, first):
         for side in range(2):
@@ -313,7 +324,7 @@
             z_step(hop, sub)
             for action in after.get((hop, sub), ()):
                 action()
-    multiply(HOP3, 0)
+    multiply_urgent(HOP3)
     y_finish(1, 0)
     multiply_side(OWN, 1, 0)
     multiply_side(HOP1, 1, 0)
@@ -324,7 +335,7 @@
     multiply(HOP2, 1)
     for sub in range(8):
         z_wait(sub // 4, 4, sub)
-    multiply(LAST, 0)
+    multiply_urgent(LAST)
     multiply(HOP3, 1)
     sum_cores(LAST)
     multiply(LAST, 1)

time: 63.3 us -> 63.3 us (level)
  no operation moved by 1% of the time
where the time goes in v6:
time: 63.3 us; the launch traced here: 63 us
  Pallas kernels  62 us (98%)
  local copies, waits for them, and re-layouts  0.97 us (2%)
    pallas_call x1, Pallas kernels, on_device(): pl.pallas_call(kernel, out_shape=jax.ShapeDtypeStruct((2 * SNAP, COLS), j...  62 us

profile of v6, /device:TPU:1, one launch (start us, length us, event | category | flops | bytes accessed | tf_op | source)
XLA Modules:
  0.0 63.0 jit_solution(6948019143199046653)
XLA Ops:
  0.0 62.0 %gram.1 = f32[1024,256]{1,0:T(8,128)S(1)} custom-call(bf16[512,384]{1,0:T(8,128)(2,1)} %snap_ref.1, f32[384]{0:T(512)} %weight_ref.1), custom_call_target="tpu_custom_call" | custom-call | tf_op jit(solution)/shard_map/gram/pallas_call | solution.py:373
  62.0 1.0 %copy.4 = f32[1024,256]{1,0:T(8,128)} copy(f32[1024,256]{1,0:T(8,128)S(1)} %gram.1) | data formatting | bytes 2097152

commit v7 on v6

--- a/solution.py
+++ b/solution.py
@@ -333,13 +333,15 @@
     multiply_side(OWN, 1, 1)
     multiply_side(HOP1, 1, 1)
     multiply(HOP2, 1)
+    sum_chips(OWN)
+    sum_chips(HOP1)
     for sub in range(8):
         z_wait(sub // 4, 4, sub)
     multiply_urgent(LAST)
     multiply(HOP3, 1)
     sum_cores(LAST)
     multiply(LAST, 1)
-    for group in GROUPS:
+    for group in (HOP2, HOP3, LAST):
         sum_chips(group)
     for p in range(8):
 

time: 63.3 us -> 63.3 us (level)
  no operation moved by 1% of the time
where the time goes in v7:
time: 63.3 us; the launch traced here: 63 us
  Pallas kernels  62 us (98%)
  local copies, waits for them, and re-layouts  0.97 us (2%)
    pallas_call x1, Pallas kernels, on_device(): pl.pallas_call(kernel, out_shape=jax.ShapeDtypeStruct((2 * SNAP, COLS), j...  62 us

profile of v7, /device:TPU:1, one launch (start us, length us, event | category | flops | bytes accessed | tf_op | source)
XLA Modules:
  0.0 63.0 jit_solution(14290922200776302793)
XLA Ops:
  0.0 62.0 %gram.1 = f32[1024,256]{1,0:T(8,128)S(1)} custom-call(bf16[512,384]{1,0:T(8,128)(2,1)} %snap_ref.1, f32[384]{0:T(512)} %weight_ref.1), custom_call_target="tpu_custom_call" | custom-call | tf_op jit(solution)/shard_map/gram/pallas_call | solution.py:375
  62.0 1.0 %copy.4 = f32[1024,256]{1,0:T(8,128)} copy(f32[1024,256]{1,0:T(8,128)S(1)} %gram.1) | data formatting | bytes 2097152
